TPU v7x, 32 devices: a whole 2x2x4 slice. The times are simulated.
32 devices in a mesh: strip: 4 (over z), date: 8 (over y, x, core).
Axes of the slice: x: 2, y: 2, z: 4, core: 2. Of those that a mesh axis runs over, the one named last changes fastest.
Arguments:
- images: bfloat16 [128, 256, 128], P('date', 'strip'), may hold values from 0.19921875 to 5
- inverse_blocks: float32 [2, 8, 128, 128], P(None, 'strip', 'date'), as said below
- pair_first: int32 [256], P('date'), may hold values from 0 to 15
- pair_block: int32 [256, 1], P('date'), may hold values from 0 to 7; in each aligned block of 32 rows (0 to 31, 32 to 63, ...) at most 8 rows name the same one
- pair_second: int32 [256], P('date'), may hold values from 0 to 15
- pair_count: int32 [8], P('date'), may hold values from 8 to 32, as said below
- shifts: int32 [256, 2, 8], P('date', None, 'strip'), may hold values from -8 to 8
- anchors: int32 [8], P('strip'), may hold values from 0 to 96, as said below
Outputs:
- pair_offsets: float32 [256, 2, 8], P('date', None, 'strip')
- series: float32 [2, 8, 128], P(None, 'strip', 'date')
Inputs may be any that keep to these rules, and one draw needn't show every extreme that they name: `pair_block`: among the 32 slots of one date block at most 8 name one partner block, and some block is named that often. `pair_count`: slots 0 to count - 1 of a date block are live; slots at or past the count carry no pair, and their partner windows need not be sent. One block has all 32 live, one has 8, every other block 24 or more. `anchors`: chip q starts at column (q % 2) * 64 plus 0 to 32. `inverse_blocks`: symmetric in its last two dimensions.
All inputs are finite; a program needn't handle non-finite values.
Results may differ from a plain program's by a relative error of at most 0.008.
Values may be sent and summed in bfloat16 or wider, within the bound.
A program may use at most 64 MiB of HBM per device.

v0:
```python
import functools
import math

import jax
import jax.numpy as jnp
import numpy as np
from jax import lax
from jax.experimental import pallas as pl
from jax.experimental.pallas import tpu as pltpu
from jax.sharding import PartitionSpec as P

SMAX = 8
MESH = pl.DeviceIdType.MESH
F32, BF16 = jnp.float32, jnp.bfloat16


def make_tables(length):
    counter = np.arange(length)
    radians = (counter[:, None] * counter[None, :] % length) * (2.0 * math.pi / length)
    cosine, sine = np.cos(radians), -np.sin(radians)
    over = 2 * length
    signed = np.where(counter < length // 2, counter, counter - length)
    places = np.arange(over)
    angles = (signed[:, None] * places[None, :] % over) * (2.0 * math.pi / over)
    vcos, vsin = np.cos(angles), np.sin(angles)
    forward = np.concatenate([cosine, sine, -sine, cosine], axis=1)
    forward = np.concatenate([forward, np.zeros_like(forward)], axis=0)
    rows = np.concatenate([cosine, sine], axis=1)
    one = np.concatenate([vcos, vsin], axis=1)
    two = np.concatenate([-vsin, vcos], axis=1)
    back = np.concatenate([one, one, two, -two], axis=0)
    final = np.concatenate([vcos.T, -vsin.T], axis=1)
    return [jnp.asarray(t.astype(np.float32)).astype(BF16) for t in (forward, rows, back, final)]


def exchange(n, strips, img, tables, grid, halo, local, send, recv):
    me, strip = lax.axis_index("date"), lax.axis_index("strip")
    up, down = lax.max(strip - 1, 0), lax.min(strip + 1, strips - 1)
    dates, length = grid.shape[1:3]
    half = dates // 2
    first, second = pl.ds(0, half), pl.ds(half, dates - half)
    if n == 8:
        peers = [jnp.bitwise_xor(me, j) for j in (1, 2, 4)]
    else:
        peers = [lax.rem(me + j, n) for j in range(1, n)]
    has_up, has_down = strip > 0, strip < strips - 1

    def sent(k, src, dst, where):
        return pltpu.make_async_remote_copy(
            src_ref=src,
            dst_ref=dst,
            send_sem=send.at[k],
            recv_sem=recv.at[k],
            device_id=where,
            device_id_type=MESH,
        )

    barrier = pltpu.get_barrier_semaphore()
    for peer in peers:
        pl.semaphore_signal(barrier, inc=1, device_id={"date": peer}, device_id_type=MESH)
    for other, has in ((up, has_up), (down, has_down)):
        @pl.when(has)
        def _():
            pl.semaphore_signal(barrier, inc=1, device_id={"strip": other}, device_id_type=MESH)
    own = pltpu.make_async_copy(img, grid.at[me], local.at[0])
    own.start()
    loads = [pltpu.make_async_copy(a, b, local.at[1 + k]) for k, (a, b) in enumerate(tables)]
    for load in loads:
        load.start()
    for side, has in ((0, has_down), (1, has_up)):
        @pl.when(jnp.logical_not(has))
        def _():
            halo[me, side] = jnp.zeros(halo.shape[2:], halo.dtype)
    pl.semaphore_wait(barrier, len(peers) + has_up.astype(jnp.int32) + has_down.astype(jnp.int32))

    top, bot = img.at[:, pl.ds(0, SMAX)], img.at[:, pl.ds(length - SMAX, SMAX)]
    z_up = sent(0, top, halo.at[me, 0], {"strip": up})
    z_down = sent(1, bot, halo.at[me, 1], {"strip": down})

    def start_z():
        pl.when(has_up)(z_up.start)
        pl.when(has_down)(z_down.start)

    def got_z():
        pl.when(has_down)(z_up.wait_recv)
        pl.when(has_up)(z_down.wait_recv)

    def left_z():
        pl.when(has_up)(z_up.wait_send)
        pl.when(has_down)(z_down.wait_send)

    def settle():
        own.wait()
        for load in loads:
            load.wait()

    if n != 8:
        start_z()
        copies = []
        for j, peer in enumerate(peers):
            copies.append(sent(2 + j, img, grid.at[me], {"date": peer}))
            copies[-1].start()
        got_z()
        left_z()
        for j, peer in enumerate(peers):
            copies.append(sent(n + 1 + j, halo.at[me], halo.at[me], {"date": peer}))
            copies[-1].start()
        settle()
        yield
        yield
        yield
        for copy in copies:
            copy.wait()
        return

    core, ex, wy = ({"date": jnp.bitwise_xor(me, j)} for j in (1, 2, 4))

    def family(base, own_ref, out, one, two):
        def made(k, block, part, where, mine=False):
            src = own_ref.at[part] if mine else out.at[block, part]
            return sent(base + k, src, out.at[block, part], where)

        near_x, near_y, diag = (jnp.bitwise_xor(me, j) for j in (2, 4, 6))
        return [
            made(0, me, one, wy, True),
            made(1, me, two, wy, True),
            made(2, me, two, ex, True),
            made(3, me, one, ex, True),
            made(4, me, one, core, True),
            made(5, near_y, one, ex),
            made(6, near_y, one, core),
            made(7, near_x, two, wy),
            made(8, near_x, two, core),
            made(9, near_y, two, core),
            made(10, near_x, one, core),
            made(11, diag, one, core),
            made(12, diag, two, core),
            made(13, me, two, core, True),
        ]

    main = family(2, img, grid, first, second)
    edge = family(16, halo.at[me], halo, 0, 1)

    def run(copies, ids):
        for k in ids:
            copies[k].start()

    run(main, (0, 2))
    start_z()
    run(main, (1, 3, 4, 13))
    settle()
    yield
    got_z()
    run(edge, (0, 2, 1, 3, 4, 13))
    main[0].wait_recv()
    run(main, (5, 6))
    main[2].wait_recv()
    run(main, (7, 8))
    yield
    main[1].wait_recv()
    run(main, (9,))
    main[3].wait_recv()
    run(main, (10,))
    edge[0].wait_recv()
    run(edge, (5, 6))
    edge[2].wait_recv()
    run(edge, (7, 8))
    edge[1].wait_recv()
    run(edge, (9,))
    edge[3].wait_recv()
    run(edge, (10,))
    yield
    main[5].wait_recv()
    run(main, (11,))
    main[7].wait_recv()
    run(main, (12,))
    edge[5].wait_recv()
    run(edge, (11,))
    edge[7].wait_recv()
    run(edge, (12,))
    for k in (4, 13, 6, 8, 9, 10, 11, 12):
        main[k].wait_recv()
        edge[k].wait_recv()
    for copy in main + edge:
        copy.wait_send()
    left_z()


def pairs_kernel(
    n, strips, batch,
    first_s, block_s, second_s, count_s, shifts_s, anchors_s,
    img, forward_in, rows_in, back_in, final_in,
    offsets_out, total_out,
    forward, rows, back, final, grid_in, halo_in, partial, held_sums, local, send, recv,
    wide, far, near, spec, sums, moments, moves,
):
    dates, length, cols = grid_in.shape[1:]
    pairs, chips = first_s.shape[0], anchors_s.shape[0]
    me, strip = lax.axis_index("date"), lax.axis_index("strip")
    lane = lax.broadcasted_iota(jnp.int32, (length, cols), 1)
    has_up, has_down = strip > 0, strip < strips - 1
    tables = ((forward_in, forward), (rows_in, rows), (back_in, back), (final_in, final))
    moving = exchange(n, strips, img, tables, grid_in, halo_in, local, send, recv)
    next(moving)

    def turned(value, start):
        rolled = pltpu.roll(value, lax.rem(2 * cols - start, cols), 1)
        inside = (lane >= -start) & (lane < cols - start)
        return jnp.where(inside, rolled, 0.0).astype(BF16)

    def near_cut(d, carry):
        value = grid_in[me, d].astype(F32)
        for c in range(chips):
            near[d * chips + c] = turned(value, anchors_s[c])
        return carry

    lax.fori_loop(0, dates, near_cut, 0, unroll=8)

    def far_cut(p, carry):
        block, day = block_s[p], second_s[p]
        wide[p, pl.ds(SMAX, length)] = grid_in[block, day].astype(F32)
        for side, at, has in ((0, SMAX + length, has_down), (1, 0, has_up)):
            edge = halo_in[block, side, day].astype(F32)
            wide[p, pl.ds(at, SMAX)] = jnp.where(has, edge, 0.0)
        for c in range(chips):
            value = wide[p, pl.ds(SMAX + shifts_s[0, c, p], length)]
            far[p * chips + c] = turned(value, anchors_s[c] + shifts_s[1, c, p])
        place = lax.broadcasted_iota(jnp.int32, (1, cols), 1)
        row = jnp.zeros((1, cols), F32)
        for x in range(2):
            for c in range(chips):
                row = jnp.where(place == x * chips + c, shifts_s[x, c, p].astype(F32), row)
        row = jnp.where(place == 2 * chips, (block * dates + day).astype(F32), row)
        row = jnp.where(place == 2 * chips + 1, (me * dates + first_s[p]).astype(F32), row)
        moves[pl.ds(p, 1)] = row
        return carry

    width = 2 * length
    lanes2 = lax.broadcasted_iota(jnp.int32, (1, 2 * width), 1)
    base = jnp.where((lanes2 == 0) | (lanes2 == width + length), 1.0 / length, 0.0)

    def spectra(ref, at, many):
        windows = ref[pl.ds(at, many)].reshape(many * length, cols)
        section = jnp.dot(windows, forward[...], preferred_element_type=F32)
        stacked = []
        for w in range(many):
            part = section[w * length:(w + 1) * length]
            part = (part - jnp.sum(part, axis=0, keepdims=True) * base).astype(BF16)
            stacked.append(jnp.concatenate([part[:, :width], part[:, width:]], axis=0))
        return jnp.dot(
            rows[...], jnp.concatenate(stacked, axis=1), preferred_element_type=F32
        )

    many = batch * chips

    def near_turn(t, carry):
        found = spectra(near, t * many, many)
        for w in range(many):
            value = found[:, w * width:(w + 1) * width]
            both = jnp.concatenate([value, pltpu.roll(value, length, 1)], axis=1)
            spec[t * many + w] = both.astype(BF16)
        return carry

    rounds = dates // batch
    next(moving)
    lax.fori_loop(0, rounds // 2, near_turn, 0)
    next(moving)
    lax.fori_loop(rounds // 2, rounds, near_turn, 0)
    for _ in moving:
        pass
    lax.fori_loop(0, pairs, far_cut, 0, unroll=32)

    steps = lax.broadcasted_iota(jnp.int32, (width, 1), 0)
    down_k = jnp.where(steps < length, steps, steps - width).astype(F32) * 0.5
    down_k = jnp.broadcast_to(down_k, (width, width))

    def turn(t, carry):
        found = spectra(far, t * many, many).astype(BF16)
        crossed = []
        for b in range(batch):
            day = first_s[t * batch + b]
            for c in range(chips):
                w = b * chips + c
                value = found[:, w * width:(w + 1) * width]
                crossed.append(spec[day * chips + c] * jnp.concatenate([value, value], axis=1))
        along = jnp.dot(
            jnp.concatenate(crossed, axis=0), back[...], preferred_element_type=F32
        ).astype(BF16)
        stacked = []
        for w in range(many):
            part = along[w * length:(w + 1) * length]
            stacked.append(jnp.concatenate([part[:, :width], part[:, width:]], axis=0))
        surface = jnp.dot(
            final[...], jnp.concatenate(stacked, axis=1), preferred_element_type=F32
        )
        for b in range(batch):
            for c in range(chips):
                w = b * chips + c
                value = surface[:, w * width:(w + 1) * width]
                energy = value * value
                at = (c, pl.ds(t * batch + b, 1))
                sums[at] = jnp.sum(energy, axis=0, keepdims=True)
                moments[at] = jnp.sum(energy * down_k, axis=0, keepdims=True)
        return carry

    lax.fori_loop(0, pairs // batch, turn, 0, unroll=2)

    across = lax.broadcasted_iota(jnp.int32, (pairs, width), 1)
    across = jnp.where(across < length, across, across - width).astype(F32) * 0.5
    live = lax.broadcasted_iota(jnp.int32, (pairs, 1), 0) < count_s[0]
    cells = 1.0 / (width * width)
    shift_all = moves[...]
    spot = lax.broadcasted_iota(jnp.int32, (pairs, partial.shape[1]), 1).astype(F32)
    spread = (spot == shift_all[:, 2 * chips:2 * chips + 1]).astype(F32) - (
        spot == shift_all[:, 2 * chips + 1:2 * chips + 2]
    ).astype(F32)
    columns = [None] * (2 * chips)
    for c in range(chips):
        held = sums[c]
        scale = jnp.sum(held, axis=1, keepdims=True) * cells + 1e-6
        low = jnp.sum(moments[c], axis=1, keepdims=True) * cells
        side = jnp.sum(held * across, axis=1, keepdims=True) * cells
        for x, value in enumerate((low, side)):
            k = x * chips + c
            columns[k] = jnp.where(live, shift_all[:, k:k + 1] + value / scale, 0.0)
    place = lax.broadcasted_iota(jnp.int32, (pairs, width), 1)
    table = jnp.zeros((pairs, width), F32)
    for k, column in enumerate(columns):
        table = jnp.where(place == k, column, table)
        partial[k:k + 1] = jnp.sum(column * spread, axis=0, keepdims=True)
    turned_table = jnp.transpose(table)
    for x in range(2):
        offsets_out[x] = turned_table[x * chips:(x + 1) * chips]

    peers = [lax.rem(me + j, n) for j in range(1, n)]
    copies = []
    for j, peer in enumerate(peers):
        copies.append(
            pltpu.make_async_remote_copy(
                src_ref=partial,
                dst_ref=held_sums.at[j],
                send_sem=send.at[send.shape[0] - n + 1 + j],
                recv_sem=recv.at[recv.shape[0] - n + 1 + j],
                device_id={"date": peer},
                device_id_type=MESH,
            )
        )
        copies[-1].start()
    total = partial[...]
    for j, copy in enumerate(copies):
        copy.wait_recv()
        total = total + held_sums[j]
    total_out[...] = total
    for copy in copies:
        copy.wait_send()


def series_kernel(total, inverse, offsets, series_out, offsets_out):
    offsets_out[...] = offsets[...]
    chips = series_out.shape[1]
    for k in range(inverse.shape[0]):
        value = jnp.sum(inverse[k] * total[k:k + 1], axis=1)[None]
        series_out[k // chips, k % chips:k % chips + 1] = value


def body(n, strips, images, inverse, first, block, second, count, shifts, anchors):
    dates, length, cols = images.shape
    pairs, chips = first.shape[0], anchors.shape[0]
    vmem, smem = pl.BlockSpec(memory_space=pltpu.VMEM), pl.BlockSpec(memory_space=pltpu.SMEM)
    tables = make_tables(length)
    kinds = (30 if n == 8 else 2 * n) + n - 1
    width = 2 * length
    batch = math.gcd(16, math.gcd(pairs, dates))
    offsets, total = pl.pallas_call(
        functools.partial(pairs_kernel, n, strips, batch),
        name="pairs",
        out_shape=(
            jax.ShapeDtypeStruct((2, chips, pairs), F32),
            jax.ShapeDtypeStruct((2 * chips, n * dates), F32),
        ),
        in_specs=[smem] * 6 + [pl.BlockSpec(memory_space=pl.ANY)] * 5,
        out_specs=(vmem, vmem),
        scratch_shapes=[
            *[pltpu.VMEM(table.shape, BF16) for table in tables],
            pltpu.VMEM((n, dates, length, cols), BF16),
            pltpu.VMEM((n, 2, dates, SMAX, cols), BF16),
            pltpu.VMEM((2 * chips, n * dates), F32),
            pltpu.VMEM((n - 1, 2 * chips, n * dates), F32),
            pltpu.SemaphoreType.DMA((1 + len(tables),)),
            pltpu.SemaphoreType.DMA((kinds,)),
            pltpu.SemaphoreType.DMA((kinds,)),
            pltpu.VMEM((pairs, length + 2 * SMAX, cols), F32),
            pltpu.VMEM((pairs * chips, length, cols), BF16),
            pltpu.VMEM((dates * chips, length, cols), BF16),
            pltpu.VMEM((dates * chips, length, 2 * width), BF16),
            pltpu.VMEM((chips, pairs, width), F32),
            pltpu.VMEM((chips, pairs, width), F32),
            pltpu.VMEM((pairs, cols), F32),
        ],
        compiler_params=pltpu.CompilerParams(collective_id=0, has_side_effects=True),
    )(
        first, block.reshape(pairs), second, count, jnp.transpose(shifts, (1, 2, 0)), anchors,
        images, *tables,
    )
    share = inverse.shape[2]
    series, offsets = pl.pallas_call(
        series_kernel,
        name="series",
        out_shape=(
            jax.ShapeDtypeStruct((2, chips, share), F32),
            jax.ShapeDtypeStruct((2, chips, pairs), F32),
        ),
        in_specs=[vmem] * 3,
        out_specs=(vmem, vmem),
    )(total, inverse.reshape(2 * chips, share, n * dates), offsets)
    return jnp.transpose(offsets, (2, 0, 1)), series


def solution(mesh):
    return jax.shard_map(
        functools.partial(body, mesh.shape["date"], mesh.shape["strip"]),
        mesh=mesh,
        in_specs=(
            P("date", "strip", None),
            P(None, "strip", "date", None),
            P("date"),
            P("date", None),
            P("date"),
            P("date"),
            P("date", None, "strip"),
            P("strip"),
        ),
        out_specs=(P("date", None, "strip"), P(None, "strip", "date")),
        check_vma=False,
    )
```

profile of v0, /device:TPU:0, one launch (start us, length us, event | category | flops | bytes accessed | tf_op | source)
XLA Modules:
  0.0 28.1 jit_solution(4936734928309026987)
XLA Ops:
  1.3 25.4 %pairs.1 = (f32[2,2,32]{2,1,0:T(2,128)}, f32[4,128]{1,0:T(4,128)}) custom-call(s32[32]{0:T(128)} %first_s.1, s32[32]{0:T(128)} %bitcast.6, s32[32]{0:T(128)} %second_s.1, s32[1]{0:T(128)S(6)} %copy.14.count_s, s32[2,2,32]{2,1,0:T(2,128)} %bitcast.5, s32[2]{0:T(128)} %anchors_s.1, bf16[16,64,128]{2,1,0:T(8,128)(2,1)} %img.1, ...), custom_call_target="tpu_custom_call" | custom-call | tf_op jit(solution)/shard_map/pairs/pallas_call | solution.py:374
  26.7 1.4 %series.1 = (f32[2,2,16]{2,1,0:T(2,128)}, f32[2,2,32]{2,1,0:T(2,128)}) custom-call(f32[4,128]{1,0:T(4,128)} %get-tuple-element.6.total, f32[4,16,128]{2,1,0:T(8,128)} %bitcast.4, f32[2,2,32]{2,1,0:T(2,128)} %get-tuple-element.7.offsets), custom_call_target="tpu_custom_call" | custom-call | tf_op jit(solution)/shard_map/series/pallas_call | solution.py:406
where the time goes:
time: 28.3 us; the launch traced here: 28.1 us
  Pallas kernels  26.8 us (95%)
  between operations  1.29 us (5%)
    pallas_call x1, Pallas kernels, body(): pl.pallas_call(functools.partial(pairs_kernel, n, strips, batch), name='p...  25.4 us
    pallas_call x1, Pallas kernels, body(): pl.pallas_call(series_kernel, name='series', out_shape=(jax.ShapeDtypeStr...  1.43 us

commit v1 on v0

v1 whole, which is shorter than its diff:
```python
import functools
import math

import jax
import jax.numpy as jnp
import numpy as np
from jax import lax
from jax.experimental import pallas as pl
from jax.experimental.pallas import tpu as pltpu
from jax.sharding import PartitionSpec as P

SMAX = 8
MESH = pl.DeviceIdType.MESH
F32, BF16, I32 = jnp.float32, jnp.bfloat16, jnp.int32


def make_tables(length):
    counter = np.arange(length)
    radians = (counter[:, None] * counter[None, :] % length) * (2.0 * math.pi / length)
    cosine, sine = np.cos(radians), -np.sin(radians)
    over = 2 * length
    signed = np.where(counter < length // 2, counter, counter - length)
    places = np.arange(over)
    angles = (signed[:, None] * places[None, :] % over) * (2.0 * math.pi / over)
    vcos, vsin = np.cos(angles), np.sin(angles)
    forward = np.concatenate([cosine, sine, -sine, cosine], axis=1)
    forward = np.concatenate([forward, np.zeros_like(forward)], axis=0)
    rows = np.concatenate([cosine, sine], axis=1)
    one = np.concatenate([vcos, vsin], axis=1)
    two = np.concatenate([-vsin, vcos], axis=1)
    back = np.concatenate([one, one, two, -two], axis=0)
    final = np.concatenate([vcos.T, -vsin.T], axis=1)
    return [jnp.asarray(t.astype(np.float32)).astype(BF16) for t in (forward, rows, back, final)]


def remote(k, src, dst, where, send, recv):
    return pltpu.make_async_remote_copy(
        src_ref=src,
        dst_ref=dst,
        send_sem=send.at[k],
        recv_sem=recv.at[k],
        device_id=where,
        device_id_type=MESH,
    )


class Gather:
    def __init__(self, me, strip, strips, blocks, send, recv):
        self.blocks = blocks
        groups = blocks[0].shape[0]
        half = (groups - 2) // 2
        last = groups - 2
        self.has_up, self.has_down = strip > 0, strip < strips - 1
        up, down = lax.max(strip - 1, 0), lax.min(strip + 1, strips - 1)
        to = {j: jnp.bitwise_xor(me, j) for j in (1, 2, 4)}
        self.to, self.up, self.down = to, up, down
        self.copies = {}
        self.kinds = 0

        def add(name, d, at, many, where, target, dst_at=None):
            dst_at = at if dst_at is None else dst_at
            copy = remote(
                self.kinds,
                blocks[d].at[pl.ds(at, many)],
                blocks[target].at[pl.ds(dst_at, many)],
                where,
                send,
                recv,
            )
            self.copies[name] = copy
            self.kinds += 1

        one, two = (1, half), (1 + half, half)
        one_edge, one_rest = (1, 1), (2, half - 1)
        two_edge, two_rest = (last, 1), (1 + half, half - 1)
        for link, first, edge, rest, relayed, r_edge, r_rest in (
            (4, one, two_edge, two_rest, 2, two_edge, two_rest),
            (2, two, one_edge, one_rest, 4, one_edge, one_rest),
        ):
            where = {"date": to[link]}
            add((link, "first"), 0, *first, where, link)
            add((link, "edge"), 0, *edge, where, link)
            add((link, "rest"), 0, *rest, where, link)
            add((link, "relay_edge"), relayed, *r_edge, where, 6)
            add((link, "relay_rest"), relayed, *r_rest, where, 6)
        where = {"date": to[1]}
        add("core", 0, 1, 2 * half, where, 1)
        for d in (2, 4, 6):
            add(("core", d, "one"), d, *one, where, d ^ 1)
            add(("core", d, "two"), d, *two, where, d ^ 1)
        for d in (0, 2, 4, 6):
            for flip in (0, 1):
                spot = {"date": jnp.bitwise_xor(me, flip)} if flip else {}
                add(("up", d, flip), d, 1, 1, {"strip": up, **spot}, d ^ flip, groups - 1)
                add(("down", d, flip), d, last, 1, {"strip": down, **spot}, d ^ flip, 0)

    def start(self, *names):
        for name in names:
            self.copies[name].start()

    def got(self, *names):
        for name in names:
            self.copies[name].wait_recv()

    def z_start(self, side, d):
        has = self.has_up if side == "up" else self.has_down

        @pl.when(has)
        def _():
            for flip in (0, 1):
                self.copies[(side, d, flip)].start()

    def z_got(self, d, flips=(0, 1)):
        @pl.when(self.has_down)
        def _():
            for flip in flips:
                self.copies[("up", d, flip)].wait_recv()

        @pl.when(self.has_up)
        def _():
            for flip in flips:
                self.copies[("down", d, flip)].wait_recv()

    def left(self):
        for name, copy in self.copies.items():
            if name[0] == "up":
                pl.when(self.has_up)(copy.wait_send)
            elif name[0] == "down":
                pl.when(self.has_down)(copy.wait_send)
            else:
                copy.wait_send()


def plain_gather(n, me, strip, strips, grid, send, recv):
    groups = grid.shape[1]
    has_up, has_down = strip > 0, strip < strips - 1
    up, down = lax.max(strip - 1, 0), lax.min(strip + 1, strips - 1)
    z_up = remote(0, grid.at[me, 1], grid.at[me, groups - 1], {"strip": up}, send, recv)
    z_down = remote(1, grid.at[me, groups - 2], grid.at[me, 0], {"strip": down}, send, recv)
    pl.when(has_up)(z_up.start)
    pl.when(has_down)(z_down.start)
    copies = []
    peers = [{"date": lax.rem(me + j, n)} for j in range(1, n)]
    main = pl.ds(1, groups - 2)
    for j, peer in enumerate(peers):
        part = grid.at[me, main]
        copies.append(remote(2 + j, part, part, peer, send, recv))
        copies[-1].start()
    pl.when(has_down)(z_up.wait_recv)
    pl.when(has_up)(z_down.wait_recv)
    pl.when(has_up)(z_up.wait_send)
    pl.when(has_down)(z_down.wait_send)
    for side, at in ((0, 0), (1, groups - 1)):
        for j, peer in enumerate(peers):
            part = grid.at[me, at]
            copies.append(remote(2 + (1 + side) * (n - 1) + j, part, part, peer, send, recv))
            copies[-1].start()
    for copy in copies:
        copy.wait()


def pairs_kernel(
    n, strips, cap,
    first_h, block_h, second_h, count_h, shifts_h, anchors_h,
    img, inverse_h, forward_h, rows_h, back_h, final_h,
    offsets_out, series_out,
    first_s, block_s, second_s, count_s, shifts_s, anchors_s, perm_s,
    first_v, block_v, second_v, shifts_v, inverse, forward, rows, back, final,
    grid, late_a, late_b, partial, held_sums,
    local, send, recv,
    wide, far, near, spec, sums, moments, picked, spread_v, columns_v, perm_v,
):
    groups, dates, _, cols = grid.shape[1:]
    length = SMAX * (groups - 2)
    pairs, chips = first_s.shape[1], anchors_s.shape[0]
    fast = n == 8
    me, strip = lax.axis_index("date"), lax.axis_index("strip")
    has_up, has_down = strip > 0, strip < strips - 1
    up, down = lax.max(strip - 1, 0), lax.min(strip + 1, strips - 1)

    barrier = pltpu.get_barrier_semaphore()
    if fast:
        greeted = [{"date": jnp.bitwise_xor(me, j)} for j in (1, 2, 4)]
        side_spots = [{}, {"date": jnp.bitwise_xor(me, 1)}]
    else:
        greeted = [{"date": lax.rem(me + j, n)} for j in range(1, n)]
        side_spots = [{}]
    for where in greeted:
        pl.semaphore_signal(barrier, inc=1, device_id=where, device_id_type=MESH)
    for other, has in ((up, has_up), (down, has_down)):
        @pl.when(has)
        def _():
            for spot in side_spots:
                pl.semaphore_signal(
                    barrier, inc=1, device_id={"strip": other, **spot}, device_id_type=MESH
                )

    count = iter(range(local.shape[0]))

    def load(src, dst):
        copy = pltpu.make_async_copy(src, dst, local.at[next(count)])
        copy.start()
        return copy

    own = 0 if fast else me
    mine = [load(img.at[:, g], grid.at[own, 1 + g]) for g in range(groups - 2)]
    small = [
        load(a, b)
        for a, b in (
            (first_h, first_s), (block_h, block_s), (second_h, second_s), (count_h, count_s),
            (shifts_h, shifts_s), (anchors_h, anchors_s),
            (first_h, first_v), (block_h, block_v), (second_h, second_v), (shifts_h, shifts_v),
        )
    ]
    large = [
        load(a, b)
        for a, b in (
            (forward_h, forward), (rows_h, rows), (back_h, back), (final_h, final),
            (inverse_h, inverse),
        )
    ]
    sides = len(side_spots) * (has_up.astype(I32) + has_down.astype(I32))
    pl.semaphore_wait(barrier, len(greeted) + sides)
    for copy in mine:
        copy.wait()
    if fast:
        blocks = [grid.at[d] for d in range(6)] + [late_a, late_b]
        move = Gather(me, strip, strips, blocks, send, recv)
        move.start((4, "first"), (2, "first"))
        move.z_start("up", 0)
        move.z_start("down", 0)
        move.start((4, "edge"), (2, "edge"), (4, "rest"), (2, "rest"), "core")
    for copy in small + large:
        copy.wait()

    line = lax.broadcasted_iota(I32, (pairs, pairs), 0)
    place = lax.broadcasted_iota(I32, (pairs, pairs), 1)
    if fast:
        distance = jnp.bitwise_xor(block_v[...], me)
        key = jnp.broadcast_to(jnp.maximum(distance - 5, 0), (pairs, pairs))
        key_line = jnp.sum(jnp.where(line == place, key, 0), axis=1, keepdims=True)
        ahead = (key < key_line) | ((key == key_line) & (place < line))
        rank_line = jnp.sum(ahead.astype(I32), axis=1, keepdims=True)
        behind = (key_line < key) | ((key_line == key) & (line < place))
        rank = jnp.sum(behind.astype(I32), axis=0, keepdims=True)
        perm_v[...] = jnp.sum(jnp.where(rank_line == place, line, 0), axis=0, keepdims=True)
        ordered = load(perm_v, perm_s)
        pick = (jnp.broadcast_to(rank, (pairs, pairs)) == line).astype(F32)
    else:
        pick = (line == place).astype(F32)
    picked[...] = pick

    def chosen(row):
        return jnp.sum(pick * row, axis=1, keepdims=True)

    spot = lax.broadcasted_iota(I32, (pairs, partial.shape[1]), 1).astype(F32)
    to_date = chosen((block_v[...] * dates + second_v[...]).astype(F32))
    from_date = chosen((me * dates + first_v[...]).astype(F32))
    spread_v[...] = (spot == to_date).astype(F32) - (spot == from_date).astype(F32)
    live = (lax.broadcasted_iota(I32, (1, pairs), 1) < count_s[0]).astype(F32)
    at = lax.broadcasted_iota(I32, columns_v.shape, 1)
    held_columns = jnp.where(at == 2 * chips, chosen(live), 0.0)
    for x in range(2):
        for c in range(chips):
            column = chosen(shifts_v[x, c:c + 1].astype(F32))
            held_columns = jnp.where(at == x * chips + c, column, held_columns)
    columns_v[...] = held_columns

    lane = lax.broadcasted_iota(I32, (length, cols), 1)

    def turned(value, start):
        rolled = pltpu.roll(value, lax.rem(2 * cols - start, cols), 1)
        inside = (lane >= -start) & (lane < cols - start)
        return jnp.where(inside, rolled, 0.0).astype(BF16)

    width = 2 * length
    lanes2 = lax.broadcasted_iota(I32, (1, 2 * width), 1)
    base = jnp.where((lanes2 == 0) | (lanes2 == width + length), 1.0 / length, 0.0)

    def spectra(ref, at, many):
        windows = ref[pl.ds(at, many)].reshape(many * length, cols)
        section = jnp.dot(windows, forward[...], preferred_element_type=F32)
        stacked = []
        for w in range(many):
            part = section[w * length:(w + 1) * length]
            part = (part - jnp.sum(part, axis=0, keepdims=True) * base).astype(BF16)
            stacked.append(jnp.concatenate([part[:, :width], part[:, width:]], axis=0))
        return jnp.dot(
            rows[...], jnp.concatenate(stacked, axis=1), preferred_element_type=F32
        )

    def near_part(low, high):
        for d in range(low, high):
            value = grid[own, pl.ds(1, groups - 2), d].astype(F32).reshape(length, cols)
            for c in range(chips):
                near[d * chips + c] = turned(value, anchors_s[c])
        many = (high - low) * chips
        found = spectra(near, low * chips, many)
        for w in range(many):
            value = found[:, w * width:(w + 1) * width]
            both = jnp.concatenate([value, pltpu.roll(value, length, 1)], axis=1)
            spec[low * chips + w] = both.astype(BF16)

    def far_cut(i, stage):
        p = perm_s[0, i] if fast else i
        block, day = block_s[0, p], second_s[0, p]
        if fast:
            distance = jnp.bitwise_xor(block, me)
            value = grid[jnp.where(distance < 6, distance, 0), :, day].astype(F32)
            if stage > 1:
                value = jnp.where(distance == 6, late_a[:, day].astype(F32), value)
            if stage > 2:
                value = jnp.where(distance == 7, late_b[:, day].astype(F32), value)
        else:
            value = grid[block, :, day].astype(F32)
        wide[i, pl.ds(0, SMAX)] = jnp.where(has_up, value[0], 0.0)
        wide[i, pl.ds(SMAX, length)] = value[1:groups - 1].reshape(length, cols)
        wide[i, pl.ds(SMAX + length, SMAX)] = jnp.where(has_down, value[groups - 1], 0.0)
        for c in range(chips):
            window = wide[i, pl.ds(SMAX + shifts_s[0, c, p], length)]
            far[i * chips + c] = turned(window, anchors_s[c] + shifts_s[1, c, p])
        return first_s[0, p]

    steps = lax.broadcasted_iota(I32, (width, 1), 0)
    down_k = jnp.where(steps < length, steps, steps - width).astype(F32) * 0.5
    down_k = jnp.broadcast_to(down_k, (width, width))

    def far_part(low, high, stage):
        days = [far_cut(i, stage) for i in range(low, high)]
        many = (high - low) * chips
        found = spectra(far, low * chips, many).astype(BF16)
        crossed = []
        for b, day in enumerate(days):
            for c in range(chips):
                w = b * chips + c
                value = found[:, w * width:(w + 1) * width]
                crossed.append(spec[day * chips + c] * jnp.concatenate([value, value], axis=1))
        along = jnp.dot(
            jnp.concatenate(crossed, axis=0), back[...], preferred_element_type=F32
        ).astype(BF16)
        stacked = []
        for w in range(many):
            part = along[w * length:(w + 1) * length]
            stacked.append(jnp.concatenate([part[:, :width], part[:, width:]], axis=0))
        surface = jnp.dot(
            final[...], jnp.concatenate(stacked, axis=1), preferred_element_type=F32
        )
        for b in range(high - low):
            for c in range(chips):
                w = b * chips + c
                value = surface[:, w * width:(w + 1) * width]
                energy = value * value
                at = (c, pl.ds(low + b, 1))
                sums[at] = jnp.sum(energy, axis=0, keepdims=True)
                moments[at] = jnp.sum(energy * down_k, axis=0, keepdims=True)

    middle = dates // 2
    if fast:
        near_part(0, middle)
        move.got((2, "first"))
        move.start((4, "relay_edge"))
        move.z_start("down", 2)
        move.got((4, "first"))
        move.start((2, "relay_edge"))
        move.z_start("up", 4)
        move.start((4, "relay_rest"), (2, "relay_rest"), ("core", 2, "two"), ("core", 4, "one"))
        near_part(middle, dates)
        move.got((2, "edge"))
        move.z_start("up", 2)
        move.got((4, "edge"))
        move.z_start("down", 4)
        ordered.wait()
        move.got((2, "rest"))
        move.start(("core", 2, "one"))
        move.got((4, "rest"))
        move.start(("core", 4, "two"))
        move.got((2, "relay_edge"))
        move.z_start("up", 6)
        move.got((4, "relay_edge"))
        move.z_start("down", 6)
        move.got("core", ("core", 2, "one"), ("core", 2, "two"))
        move.got(("core", 4, "one"), ("core", 4, "two"))
        for d in (0, 2, 4):
            move.z_got(d)
        far_part(0, pairs - 2 * cap, 1)
        move.got((2, "relay_rest"))
        move.start(("core", 6, "one"))
        move.got((4, "relay_rest"))
        move.start(("core", 6, "two"))
        move.z_got(6, (0,))
        far_part(pairs - 2 * cap, pairs - cap, 2)
        move.got(("core", 6, "one"), ("core", 6, "two"))
        move.z_got(6, (1,))
        far_part(pairs - cap, pairs, 3)
        sent = move.kinds
    else:
        near_part(0, middle)
        near_part(middle, dates)
        plain_gather(n, me, strip, strips, grid, send, recv)
        far_part(0, pairs, 1)
        sent = 2 + 3 * (n - 1)

    across = lax.broadcasted_iota(I32, (pairs, width), 1)
    across = jnp.where(across < length, across, across - width).astype(F32) * 0.5
    cells = 1.0 / (width * width)
    held_columns = columns_v[...]
    lives = held_columns[:, 2 * chips:2 * chips + 1] > 0.5
    spread = spread_v[...]
    found = [None] * (2 * chips)
    for c in range(chips):
        held = sums[c]
        scale = jnp.sum(held, axis=1, keepdims=True) * cells + 1e-6
        low = jnp.sum(moments[c], axis=1, keepdims=True) * cells
        side = jnp.sum(held * across, axis=1, keepdims=True) * cells
        for x, value in enumerate((low, side)):
            k = x * chips + c
            found[k] = jnp.where(lives, held_columns[:, k:k + 1] + value / scale, 0.0)
            partial[k:k + 1] = jnp.sum(found[k] * spread, axis=0, keepdims=True)

    copies = []
    for j in range(1, n):
        where = {"date": lax.rem(me + j, n)}
        copies.append(remote(sent + j - 1, partial, held_sums.at[j - 1], where, send, recv))
        copies[-1].start()
    pick = picked[...]
    for x in range(2):
        for c in range(chips):
            offsets_out[x, c:c + 1] = jnp.sum(found[x * chips + c] * pick, axis=0, keepdims=True)
    total = partial[...]
    for j, copy in enumerate(copies):
        copy.wait_recv()
        total = total + held_sums[j]
    for x in range(2):
        for c in range(chips):
            k = x * chips + c
            value = jnp.sum(inverse[k] * total[k:k + 1], axis=1)[None]
            series_out[x, c:c + 1] = value
    if fast:
        move.left()
    for copy in copies:
        copy.wait_send()


def emit_kernel(offsets, series, offsets_out, series_out, done):
    copies = [
        pltpu.make_async_copy(a, b, done.at[k])
        for k, (a, b) in enumerate(((offsets, offsets_out), (series, series_out)))
    ]
    for copy in copies:
        copy.start()
    for copy in copies:
        copy.wait()


def body(n, strips, images, inverse, first, block, second, count, shifts, anchors):
    dates, length, cols = images.shape
    pairs, chips = first.shape[0], anchors.shape[0]
    vmem, anywhere = pl.BlockSpec(memory_space=pltpu.VMEM), pl.BlockSpec(memory_space=pl.ANY)
    tables = make_tables(length)
    fast = n == 8
    kinds = (33 if fast else 2 + 3 * (n - 1)) + n - 1
    width = 2 * length
    cap = 2 * pairs // n
    groups = length // SMAX + 2
    share = inverse.shape[2]
    block_shape = (groups, dates, SMAX, cols)
    late = block_shape if fast else (SMAX, cols)
    offsets, series = pl.pallas_call(
        functools.partial(pairs_kernel, n, strips, cap),
        name="pairs",
        out_shape=(
            pltpu.VMEM((2, chips, pairs), F32),
            pltpu.VMEM((2, chips, share), F32),
        ),
        in_specs=[anywhere] * 12,
        out_specs=(vmem, vmem),
        scratch_shapes=[
            pltpu.SMEM((1, pairs), I32),
            pltpu.SMEM((1, pairs), I32),
            pltpu.SMEM((1, pairs), I32),
            pltpu.SMEM((1,), I32),
            pltpu.SMEM((2, chips, pairs), I32),
            pltpu.SMEM((chips,), I32),
            pltpu.SMEM((1, pairs), I32),
            pltpu.VMEM((1, pairs), I32),
            pltpu.VMEM((1, pairs), I32),
            pltpu.VMEM((1, pairs), I32),
            pltpu.VMEM((2, chips, pairs), I32),
            pltpu.VMEM((2 * chips, share, n * dates), F32),
            *[pltpu.VMEM(table.shape, BF16) for table in tables],
            pltpu.VMEM((6 if fast else n, *block_shape), BF16),
            pltpu.VMEM(late, BF16),
            pltpu.VMEM(late, BF16),
            pltpu.VMEM((2 * chips, n * dates), F32),
            pltpu.VMEM((n - 1, 2 * chips, n * dates), F32),
            pltpu.SemaphoreType.DMA((groups + 14,)),
            pltpu.SemaphoreType.DMA((kinds,)),
            pltpu.SemaphoreType.DMA((kinds,)),
            pltpu.VMEM((pairs, length + 2 * SMAX, cols), F32),
            pltpu.VMEM((pairs * chips, length, cols), BF16),
            pltpu.VMEM((dates * chips, length, cols), BF16),
            pltpu.VMEM((dates * chips, length, 2 * width), BF16),
            pltpu.VMEM((chips, pairs, width), F32),
            pltpu.VMEM((chips, pairs, width), F32),
            pltpu.VMEM((pairs, pairs), F32),
            pltpu.VMEM((pairs, n * dates), F32),
            pltpu.VMEM((pairs, cols), F32),
            pltpu.VMEM((1, pairs), I32),
        ],
        compiler_params=pltpu.CompilerParams(collective_id=0, has_side_effects=True),
    )(
        first.reshape(1, pairs), block.reshape(1, pairs), second.reshape(1, pairs), count,
        jnp.transpose(shifts, (1, 2, 0)), anchors,
        images.reshape(dates, length // SMAX, SMAX, cols),
        inverse.reshape(2 * chips, share, n * dates), *tables,
    )
    offsets, series = pl.pallas_call(
        emit_kernel,
        name="emit",
        out_shape=(
            jax.ShapeDtypeStruct(offsets.shape, F32),
            jax.ShapeDtypeStruct(series.shape, F32),
        ),
        in_specs=[vmem] * 2,
        out_specs=(anywhere, anywhere),
        scratch_shapes=[pltpu.SemaphoreType.DMA((2,))],
    )(
        pltpu.with_memory_space_constraint(offsets, pltpu.VMEM),
        pltpu.with_memory_space_constraint(series, pltpu.VMEM),
    )
    return jnp.transpose(offsets, (2, 0, 1)), series


def solution(mesh):
    return jax.shard_map(
        functools.partial(body, mesh.shape["date"], mesh.shape["strip"]),
        mesh=mesh,
        in_specs=(
            P("date", "strip", None),
            P(None, "strip", "date", None),
            P("date"),
            P("date", None),
            P("date"),
            P("date"),
            P("date", None, "strip"),
            P("strip"),
        ),
        out_specs=(P("date", None, "strip"), P(None, "strip", "date")),
        check_vma=False,
    )
```

time: 28.3 us -> 24.8 us (0.88)
  Pallas kernels: 26.8 us -> 23.4 us
    pallas_call x2, Pallas kernels: 26.8 us -> 23.4 us  [the longest x1 22.8 us: body(): pl.pallas_call(functools.partial(pairs_kernel, n, strips, cap), name='pai...]
where the time goes in v1:
time: 24.8 us; the launch traced here: 24.7 us
  Pallas kernels  23.4 us (94%)
  between operations  1.29 us (5%)
    pallas_call x1, Pallas kernels, body(): pl.pallas_call(functools.partial(pairs_kernel, n, strips, cap), name='pai...  22.8 us
    pallas_call x1, Pallas kernels, body(): pl.pallas_call(emit_kernel, name='emit', out_shape=(jax.ShapeDtypeStruct(...  0.6 us

profile of v1, /device:TPU:0, one launch (start us, length us, event | category | flops | bytes accessed | tf_op | source)
XLA Modules:
  0.0 24.7 jit_solution(14335772379063740558)
XLA Ops:
  1.3 22.8 %pairs.1 = (f32[2,2,32]{2,1,0:T(2,128)S(1)}, f32[2,2,16]{2,1,0:T(2,128)S(1)}) custom-call(s32[1,32]{1,0:T(1,128)} %bitcast.10, s32[1,32]{1,0:T(1,128)} %bitcast.11, s32[1,32]{1,0:T(1,128)} %bitcast.12, s32[1]{0:T(128)S(6)} %copy.14.count_h, s32[2,2,32]{2,1,0:T(2,128)} %bitcast.9, s32[2]{0:T(128)} %anchors_h.1, bf16[16,8,8,128]{3,2,1,0:T(8,128)(2,1)} %bitcast.7, ...), custom_call_target="tpu_custom_call" | custom-call | tf_op jit(solution)/shard_map/pairs/pallas_call | solution.py:468
  24.1 0.6 %emit.1 = (f32[2,2,32]{2,1,0:T(2,128)}, f32[2,2,16]{2,1,0:T(2,128)}) custom-call(f32[2,2,32]{2,1,0:T(2,128)S(1)} %get-tuple-element.6.offsets, f32[2,2,16]{2,1,0:T(2,128)S(1)} %get-tuple-element.7.series), custom_call_target="tpu_custom_call" | custom-call | tf_op jit(solution)/shard_map/emit/pallas_call | solution.py:517

commit v2 on v1

--- a/solution.py
+++ b/solution.py
@@ -10,6 +10,8 @@
 from jax.sharding import PartitionSpec as P
 
 SMAX = 8
+SPLIT = 8
+PIECES = 1
 MESH = pl.DeviceIdType.MESH
 F32, BF16, I32 = jnp.float32, jnp.bfloat16, jnp.int32
 
@@ -23,8 +25,9 @@
     places = np.arange(over)
     angles = (signed[:, None] * places[None, :] % over) * (2.0 * math.pi / over)
     vcos, vsin = np.cos(angles), np.sin(angles)
-    forward = np.concatenate([cosine, sine, -sine, cosine], axis=1)
-    forward = np.concatenate([forward, np.zeros_like(forward)], axis=0)
+    forward = np.concatenate([cosine, sine], axis=1)
+    empty = np.zeros_like(forward)
+    forward = np.block([[forward, empty], [empty, forward]])
     rows = np.concatenate([cosine, sine], axis=1)
     one = np.concatenate([vcos, vsin], axis=1)
     two = np.concatenate([-vsin, vcos], axis=1)
@@ -70,37 +73,47 @@
             self.copies[name] = copy
             self.kinds += 1
 
-        one, two = (1, half), (1 + half, half)
-        one_edge, one_rest = (1, 1), (2, half - 1)
-        two_edge, two_rest = (last, 1), (1 + half, half - 1)
-        for link, first, edge, rest, relayed, r_edge, r_rest in (
-            (4, one, two_edge, two_rest, 2, two_edge, two_rest),
-            (2, two, one_edge, one_rest, 4, one_edge, one_rest),
-        ):
+        edges = {"one": 1, "two": last}
+        rests = {"one": 2, "two": 1 + half}
+        inner = half - 1
+        core = {"date": to[1]}
+        add(("core", 0), 0, 1, 2 * half, core, 1)
+        for link, now, later, relayed in ((4, "one", "two", 2), (2, "two", "one", 4)):
             where = {"date": to[link]}
-            add((link, "first"), 0, *first, where, link)
-            add((link, "edge"), 0, *edge, where, link)
-            add((link, "rest"), 0, *rest, where, link)
-            add((link, "relay_edge"), relayed, *r_edge, where, 6)
-            add((link, "relay_rest"), relayed, *r_rest, where, 6)
-        where = {"date": to[1]}
-        add("core", 0, 1, 2 * half, where, 1)
-        for d in (2, 4, 6):
-            add(("core", d, "one"), d, *one, where, d ^ 1)
-            add(("core", d, "two"), d, *two, where, d ^ 1)
+            add((link, "now_edge"), 0, edges[now], 1, where, link)
+            add((link, "now_rest"), 0, rests[now], inner, where, link)
+            add((link, "later_edge"), 0, edges[later], 1, where, link)
+            add((link, "relay_edge"), relayed, edges[later], 1, where, 6)
+            begin = min(edges[now], rests[now])
+            add(("core", link, "now"), link, begin, half, core, link ^ 1)
+            add(("core", link, "edge"), link, edges[later], 1, core, link ^ 1)
+            add(("core", 6, link, "edge"), 6, edges[later], 1, core, 7)
+            for k in range(PIECES):
+                many = inner // PIECES
+                at = rests[later] + k * many
+                add((link, "later_rest", k), 0, at, many, where, link)
+                add((link, "relay_rest", k), relayed, at, many, where, 6)
+                add(("core", link, "rest", k), link, at, many, core, link ^ 1)
+                add(("core", 6, link, "rest", k), 6, at, many, core, 7)
+        self.inner = PIECES
         for d in (0, 2, 4, 6):
             for flip in (0, 1):
                 spot = {"date": jnp.bitwise_xor(me, flip)} if flip else {}
                 add(("up", d, flip), d, 1, 1, {"strip": up, **spot}, d ^ flip, groups - 1)
                 add(("down", d, flip), d, last, 1, {"strip": down, **spot}, d ^ flip, 0)
 
+    def named(self, names):
+        for key, copy in self.copies.items():
+            if key in names or key[:2] in names:
+                yield copy
+
     def start(self, *names):
-        for name in names:
-            self.copies[name].start()
+        for copy in self.named(names):
+            copy.start()
 
     def got(self, *names):
-        for name in names:
-            self.copies[name].wait_recv()
+        for copy in self.named(names):
+            copy.wait_recv()
 
     def z_start(self, side, d):
         has = self.has_up if side == "up" else self.has_down
@@ -166,9 +179,9 @@
     offsets_out, series_out,
     first_s, block_s, second_s, count_s, shifts_s, anchors_s, perm_s,
     first_v, block_v, second_v, shifts_v, inverse, forward, rows, back, final,
-    grid, late_a, late_b, partial, held_sums,
+    grid, late, partial, held_sums,
     local, send, recv,
-    wide, far, near, spec, sums, moments, picked, spread_v, columns_v, perm_v,
+    wide, far, near, spec, far_spec, sums, moments, picked, spread_v, columns_v, perm_v,
 ):
     groups, dates, _, cols = grid.shape[1:]
     length = SMAX * (groups - 2)
@@ -203,7 +216,8 @@
         return copy
 
     own = 0 if fast else me
-    mine = [load(img.at[:, g], grid.at[own, 1 + g]) for g in range(groups - 2)]
+    spots = [0, groups - 3, *range(1, groups - 3)]
+    mine = [load(img.at[:, g], grid.at[own, 1 + g]) for g in spots]
     small = [
         load(a, b)
         for a, b in (
@@ -221,15 +235,19 @@
     ]
     sides = len(side_spots) * (has_up.astype(I32) + has_down.astype(I32))
     pl.semaphore_wait(barrier, len(greeted) + sides)
-    for copy in mine:
+    for copy in mine[:2]:
         copy.wait()
     if fast:
-        blocks = [grid.at[d] for d in range(6)] + [late_a, late_b]
+        blocks = [grid.at[d] for d in range(6)] + [late.at[d] for d in range(2)]
         move = Gather(me, strip, strips, blocks, send, recv)
-        move.start((4, "first"), (2, "first"))
+        move.start((4, "now_edge"), (2, "now_edge"))
+        move.start((4, "later_edge"), (2, "later_edge"))
         move.z_start("up", 0)
         move.z_start("down", 0)
-        move.start((4, "edge"), (2, "edge"), (4, "rest"), (2, "rest"), "core")
+    for copy in mine[2:]:
+        copy.wait()
+    if fast:
+        move.start((4, "now_rest"), (2, "now_rest"), ("core", 0))
     for copy in small + large:
         copy.wait()
 
@@ -266,39 +284,53 @@
             held_columns = jnp.where(at == x * chips + c, column, held_columns)
     columns_v[...] = held_columns
 
-    lane = lax.broadcasted_iota(I32, (length, cols), 1)
-
-    def turned(value, start):
-        rolled = pltpu.roll(value, lax.rem(2 * cols - start, cols), 1)
-        inside = (lane >= -start) & (lane < cols - start)
-        return jnp.where(inside, rolled, 0.0).astype(BF16)
+    lane = lax.broadcasted_iota(I32, (1, cols), 1)
+    left_half = lane < length
+
+    def paired(one, start_one, two, start_two):
+        one = pltpu.roll(one, lax.rem(2 * cols - start_one, cols), 1)
+        two = pltpu.roll(two, lax.rem(2 * cols + length - start_two, cols), 1)
+        column = jnp.where(left_half, start_one + lane, start_two - length + lane)
+        inside = jnp.where((column >= 0) & (column < cols), 1.0, 0.0)
+        both = jnp.where(jnp.broadcast_to(left_half, one.shape), one, two)
+        return (both * inside).astype(BF16)
 
     width = 2 * length
     lanes2 = lax.broadcasted_iota(I32, (1, 2 * width), 1)
-    base = jnp.where((lanes2 == 0) | (lanes2 == width + length), 1.0 / length, 0.0)
+    base = jnp.where((lanes2 == 0) | (lanes2 == width), 1.0 / length, 0.0)
+    turn_sign = jnp.where(left_half, -1.0, 1.0).astype(BF16)
+
+    def split(many, size):
+        step = max(1, many // SPLIT) * size
+        return [(at, step) for at in range(0, many * size, step)]
 
     def spectra(ref, at, many):
         windows = ref[pl.ds(at, many)].reshape(many * length, cols)
-        section = jnp.dot(windows, forward[...], preferred_element_type=F32)
+        sections = []
+        for start, size in split(many, length):
+            found = jnp.dot(windows[start:start + size], forward[...], preferred_element_type=F32)
+            sections += [found[k:k + length] for k in range(0, size, length)]
         stacked = []
-        for w in range(many):
-            part = section[w * length:(w + 1) * length]
-            part = (part - jnp.sum(part, axis=0, keepdims=True) * base).astype(BF16)
-            stacked.append(jnp.concatenate([part[:, :width], part[:, width:]], axis=0))
-        return jnp.dot(
-            rows[...], jnp.concatenate(stacked, axis=1), preferred_element_type=F32
-        )
+        for part in sections:
+            part = part - jnp.sum(part, axis=0, keepdims=True) * base
+            for c in range(2):
+                top = part[:, c * width:(c + 1) * width]
+                low = pltpu.roll(top, length, 1).astype(BF16) * turn_sign
+                stacked.append(jnp.concatenate([top.astype(BF16), low], axis=0))
+        found = []
+        for start, size in split(many, 2):
+            both = jnp.concatenate(stacked[start:start + size], axis=1)
+            both = jnp.dot(rows[...], both, preferred_element_type=F32)
+            found += [both[:, k * width:(k + 1) * width] for k in range(size)]
+        return found
 
     def near_part(low, high):
         for d in range(low, high):
             value = grid[own, pl.ds(1, groups - 2), d].astype(F32).reshape(length, cols)
-            for c in range(chips):
-                near[d * chips + c] = turned(value, anchors_s[c])
-        many = (high - low) * chips
-        found = spectra(near, low * chips, many)
-        for w in range(many):
-            value = found[:, w * width:(w + 1) * width]
-            both = jnp.concatenate([value, pltpu.roll(value, length, 1)], axis=1)
+            near[d] = paired(value, anchors_s[0], value, anchors_s[1])
+        found = spectra(near, low, high - low)
+        for w in range((high - low) * chips):
+            both = jnp.concatenate([found[w], pltpu.roll(found[w], length, 1)], axis=1)
             spec[low * chips + w] = both.astype(BF16)
 
     def far_cut(i, stage):
@@ -308,96 +340,115 @@
             distance = jnp.bitwise_xor(block, me)
             value = grid[jnp.where(distance < 6, distance, 0), :, day].astype(F32)
             if stage > 1:
-                value = jnp.where(distance == 6, late_a[:, day].astype(F32), value)
-            if stage > 2:
-                value = jnp.where(distance == 7, late_b[:, day].astype(F32), value)
+                other = late[jnp.where(distance == 7, 1, 0), :, day].astype(F32)
+                value = jnp.where(distance < 6, value, other)
         else:
             value = grid[block, :, day].astype(F32)
         wide[i, pl.ds(0, SMAX)] = jnp.where(has_up, value[0], 0.0)
         wide[i, pl.ds(SMAX, length)] = value[1:groups - 1].reshape(length, cols)
         wide[i, pl.ds(SMAX + length, SMAX)] = jnp.where(has_down, value[groups - 1], 0.0)
-        for c in range(chips):
-            window = wide[i, pl.ds(SMAX + shifts_s[0, c, p], length)]
-            far[i * chips + c] = turned(window, anchors_s[c] + shifts_s[1, c, p])
-        return first_s[0, p]
-
-    steps = lax.broadcasted_iota(I32, (width, 1), 0)
-    down_k = jnp.where(steps < length, steps, steps - width).astype(F32) * 0.5
-    down_k = jnp.broadcast_to(down_k, (width, width))
-
-    def far_part(low, high, stage):
-        days = [far_cut(i, stage) for i in range(low, high)]
+        windows = []
+        for c in range(2):
+            windows.append(wide[i, pl.ds(SMAX + shifts_s[0, c, p], length)])
+            windows.append(anchors_s[c] + shifts_s[1, c, p])
+        far[i] = paired(*windows)
+
+    tiles = width // SMAX
+    row_in = lax.broadcasted_iota(I32, (SMAX, width), 0).astype(F32) * 0.5
+    row_in = row_in - (tiles // 2 + 1) * (SMAX // 2)
+
+    def far_spectra(low, high, stage):
+        for i in range(low, high):
+            far_cut(i, stage)
+        found = spectra(far, low, high - low)
+        for w, value in enumerate(found):
+            far_spec[low * chips + w] = value.astype(BF16)
+
+    def far_centres(low, high):
         many = (high - low) * chips
-        found = spectra(far, low * chips, many).astype(BF16)
         crossed = []
-        for b, day in enumerate(days):
+        for i in range(low, high):
+            day = first_s[0, perm_s[0, i] if fast else i]
             for c in range(chips):
-                w = b * chips + c
-                value = found[:, w * width:(w + 1) * width]
+                value = far_spec[i * chips + c]
                 crossed.append(spec[day * chips + c] * jnp.concatenate([value, value], axis=1))
-        along = jnp.dot(
-            jnp.concatenate(crossed, axis=0), back[...], preferred_element_type=F32
-        ).astype(BF16)
         stacked = []
-        for w in range(many):
-            part = along[w * length:(w + 1) * length]
-            stacked.append(jnp.concatenate([part[:, :width], part[:, width:]], axis=0))
-        surface = jnp.dot(
-            final[...], jnp.concatenate(stacked, axis=1), preferred_element_type=F32
-        )
+        for start, size in split(many, 1):
+            along = jnp.concatenate(crossed[start:start + size], axis=0)
+            along = jnp.dot(along, back[...], preferred_element_type=F32).astype(BF16)
+            for w in range(size):
+                part = along[w * length:(w + 1) * length]
+                stacked.append(jnp.concatenate([part[:, :width], part[:, width:]], axis=0))
+        surfaces = []
+        for start, size in split(many, 1):
+            both = jnp.concatenate(stacked[start:start + size], axis=1)
+            both = jnp.dot(final[...], both, preferred_element_type=F32)
+            surfaces += [both[:, k * width:(k + 1) * width] for k in range(size)]
         for b in range(high - low):
             for c in range(chips):
                 w = b * chips + c
-                value = surface[:, w * width:(w + 1) * width]
-                energy = value * value
+                value = surfaces[w]
+                run, ramp = None, None
+                for t in (*range(tiles // 2 - 1, -1, -1), *range(tiles - 1, tiles // 2 - 1, -1)):
+                    energy = value[t * SMAX:(t + 1) * SMAX]
+                    energy = energy * energy
+                    run = energy if run is None else run + energy
+                    ramp = run if ramp is None else ramp + run
                 at = (c, pl.ds(low + b, 1))
-                sums[at] = jnp.sum(energy, axis=0, keepdims=True)
-                moments[at] = jnp.sum(energy * down_k, axis=0, keepdims=True)
+                sums[at] = jnp.sum(run, axis=0, keepdims=True)
+                weighted = ramp * (SMAX // 2) + run * row_in
+                moments[at] = jnp.sum(weighted, axis=0, keepdims=True)
 
     middle = dates // 2
     if fast:
         near_part(0, middle)
-        move.got((2, "first"))
-        move.start((4, "relay_edge"))
-        move.z_start("down", 2)
-        move.got((4, "first"))
-        move.start((2, "relay_edge"))
-        move.z_start("up", 4)
-        move.start((4, "relay_rest"), (2, "relay_rest"), ("core", 2, "two"), ("core", 4, "one"))
+        for link, side in ((2, "down"), (4, "up")):
+            move.got((link, "now_edge"))
+            move.start((6 - link, "relay_edge"))
+            move.z_start(side, link)
+        move.start((4, "later_rest"), (2, "later_rest"))
+        for link, side in ((2, "up"), (4, "down")):
+            move.got((link, "later_edge"))
+            move.z_start(side, link)
+            move.start(("core", link, "edge"))
         near_part(middle, dates)
-        move.got((2, "edge"))
-        move.z_start("up", 2)
-        move.got((4, "edge"))
-        move.z_start("down", 4)
+        for link in (2, 4):
+            move.got((link, "now_rest"))
+            move.start((6 - link, "relay_rest"), ("core", link, "now"))
         ordered.wait()
-        move.got((2, "rest"))
-        move.start(("core", 2, "one"))
-        move.got((4, "rest"))
-        move.start(("core", 4, "two"))
-        move.got((2, "relay_edge"))
-        move.z_start("up", 6)
-        move.got((4, "relay_edge"))
-        move.z_start("down", 6)
-        move.got("core", ("core", 2, "one"), ("core", 2, "two"))
-        move.got(("core", 4, "one"), ("core", 4, "two"))
+        for link, side in ((2, "up"), (4, "down")):
+            move.got((link, "relay_edge"))
+            move.z_start(side, 6)
+            move.start(("core", 6, link, "edge"))
+        for k in range(move.inner):
+            for link in (2, 4):
+                move.got((link, "later_rest", k))
+                move.start(("core", link, "rest", k))
+        move.got(("core", 0), ("core", 2), ("core", 4))
         for d in (0, 2, 4):
             move.z_got(d)
-        far_part(0, pairs - 2 * cap, 1)
-        move.got((2, "relay_rest"))
-        move.start(("core", 6, "one"))
-        move.got((4, "relay_rest"))
-        move.start(("core", 6, "two"))
-        move.z_got(6, (0,))
-        far_part(pairs - 2 * cap, pairs - cap, 2)
-        move.got(("core", 6, "one"), ("core", 6, "two"))
-        move.z_got(6, (1,))
-        far_part(pairs - cap, pairs, 3)
+
+        def hand_on(*pieces):
+            for k in pieces:
+                for link in (2, 4):
+                    move.got((link, "relay_rest", k))
+                    move.start(("core", 6, link, "rest", k))
+
+        early = pairs - 2 * cap
+        far_spectra(0, early, 1)
+        hand_on(*range(move.inner))
+        far_centres(0, early)
+        move.got(("core", 6))
+        move.z_got(6)
+        far_spectra(early, pairs, 2)
+        far_centres(early, pairs)
         sent = move.kinds
     else:
         near_part(0, middle)
         near_part(middle, dates)
         plain_gather(n, me, strip, strips, grid, send, recv)
-        far_part(0, pairs, 1)
+        far_spectra(0, pairs, 1)
+        far_centres(0, pairs)
         sent = 2 + 3 * (n - 1)
 
     across = lax.broadcasted_iota(I32, (pairs, width), 1)
@@ -458,13 +509,14 @@
     vmem, anywhere = pl.BlockSpec(memory_space=pltpu.VMEM), pl.BlockSpec(memory_space=pl.ANY)
     tables = make_tables(length)
     fast = n == 8
-    kinds = (33 if fast else 2 + 3 * (n - 1)) + n - 1
+    half = length // SMAX // 2
+    kinds = (17 + 14 + 8 * PIECES if fast else 2 + 3 * (n - 1)) + n - 1
     width = 2 * length
     cap = 2 * pairs // n
     groups = length // SMAX + 2
     share = inverse.shape[2]
     block_shape = (groups, dates, SMAX, cols)
-    late = block_shape if fast else (SMAX, cols)
+    late = (2, *block_shape) if fast else (SMAX, cols)
     offsets, series = pl.pallas_call(
         functools.partial(pairs_kernel, n, strips, cap),
         name="pairs",
@@ -490,16 +542,16 @@
             *[pltpu.VMEM(table.shape, BF16) for table in tables],
             pltpu.VMEM((6 if fast else n, *block_shape), BF16),
             pltpu.VMEM(late, BF16),
-            pltpu.VMEM(late, BF16),
             pltpu.VMEM((2 * chips, n * dates), F32),
             pltpu.VMEM((n - 1, 2 * chips, n * dates), F32),
             pltpu.SemaphoreType.DMA((groups + 14,)),
             pltpu.SemaphoreType.DMA((kinds,)),
             pltpu.SemaphoreType.DMA((kinds,)),
             pltpu.VMEM((pairs, length + 2 * SMAX, cols), F32),
-            pltpu.VMEM((pairs * chips, length, cols), BF16),
-            pltpu.VMEM((dates * chips, length, cols), BF16),
+            pltpu.VMEM((pairs, length, cols), BF16),
+            pltpu.VMEM((dates, length, cols), BF16),
             pltpu.VMEM((dates * chips, length, 2 * width), BF16),
+            pltpu.VMEM((pairs * chips, length, width), BF16),
             pltpu.VMEM((chips, pairs, width), F32),
             pltpu.VMEM((chips, pairs, width), F32),
             pltpu.VMEM((pairs, pairs), F32),

time: 24.8 us -> 24 us (0.968)
  Pallas kernels: 23.4 us -> 22.5 us
    pallas_call x1, Pallas kernels: 22.8 us -> 21.9 us  [body(): pl.pallas_call(functools.partial(pairs_kernel, n, strips, cap), name='pai...]
where the time goes in v2:
time: 24 us; the launch traced here: 23.8 us
  Pallas kernels  22.5 us (94%)
  between operations  1.29 us (5%)
    pallas_call x1, Pallas kernels, body(): pl.pallas_call(functools.partial(pairs_kernel, n, strips, cap), name='pai...  21.9 us
    pallas_call x1, Pallas kernels, body(): pl.pallas_call(emit_kernel, name='emit', out_shape=(jax.ShapeDtypeStruct(...  0.6 us

profile of v2, /device:TPU:0, one launch (start us, length us, event | category | flops | bytes accessed | tf_op | source)
XLA Modules:
  0.0 23.8 jit_solution(16701998252334143613)
XLA Ops:
  1.3 21.9 %pairs.1 = (f32[2,2,32]{2,1,0:T(2,128)S(1)}, f32[2,2,16]{2,1,0:T(2,128)S(1)}) custom-call(s32[1,32]{1,0:T(1,128)} %bitcast.10, s32[1,32]{1,0:T(1,128)} %bitcast.11, s32[1,32]{1,0:T(1,128)} %bitcast.12, s32[1]{0:T(128)S(6)} %copy.14.count_h, s32[2,2,32]{2,1,0:T(2,128)} %bitcast.9, s32[2]{0:T(128)} %anchors_h.1, bf16[16,8,8,128]{3,2,1,0:T(8,128)(2,1)} %bitcast.7, ...), custom_call_target="tpu_custom_call" | custom-call | tf_op jit(solution)/shard_map/pairs/pallas_call | solution.py:520
  23.2 0.6 %emit.1 = (f32[2,2,32]{2,1,0:T(2,128)}, f32[2,2,16]{2,1,0:T(2,128)}) custom-call(f32[2,2,32]{2,1,0:T(2,128)S(1)} %get-tuple-element.6.offsets, f32[2,2,16]{2,1,0:T(2,128)S(1)} %get-tuple-element.7.series), custom_call_target="tpu_custom_call" | custom-call | tf_op jit(solution)/shard_map/emit/pallas_call | solution.py:569

commit v3 on v2

--- a/solution.py
+++ b/solution.py
@@ -28,11 +28,22 @@
     forward = np.concatenate([cosine, sine], axis=1)
     empty = np.zeros_like(forward)
     forward = np.block([[forward, empty], [empty, forward]])
-    rows = np.concatenate([cosine, sine], axis=1)
+    half = length // 2
+    kept = -(-(half + 1) // 16) * 16
+    rows = np.zeros((kept, over))
+    rows[:half + 1] = np.concatenate([cosine, sine], axis=1)[:half + 1]
+    vsin[half] = 0.0
     one = np.concatenate([vcos, vsin], axis=1)
     two = np.concatenate([-vsin, vcos], axis=1)
     back = np.concatenate([one, one, two, -two], axis=0)
-    final = np.concatenate([vcos.T, -vsin.T], axis=1)
+    lean = ((places + length) % over - length) * 0.5
+    waves = counter[:half + 1, None] * places[None, :] * (2.0 * math.pi / over)
+    even = np.where((counter[:half + 1] == 0) | (counter[:half + 1] == half), 1.0, 2.0)
+    odd = np.where(counter[:half + 1] == half, 1.0, -2.0)
+    final = np.zeros((kept, kept))
+    final[:half + 1, :half + 1] = 2.0 * (even[:, None] * np.cos(waves) * lean) @ (
+        odd[:, None] * np.sin(waves)
+    ).T
     return [jnp.asarray(t.astype(np.float32)).astype(BF16) for t in (forward, rows, back, final)]
 
 
@@ -288,12 +299,13 @@
     left_half = lane < length
 
     def paired(one, start_one, two, start_two):
-        one = pltpu.roll(one, lax.rem(2 * cols - start_one, cols), 1)
-        two = pltpu.roll(two, lax.rem(2 * cols + length - start_two, cols), 1)
+        one = pltpu.roll(one.astype(BF16), lax.rem(2 * cols - start_one, cols), 1)
+        two = pltpu.roll(two.astype(BF16), lax.rem(2 * cols + length - start_two, cols), 1)
         column = jnp.where(left_half, start_one + lane, start_two - length + lane)
-        inside = jnp.where((column >= 0) & (column < cols), 1.0, 0.0)
-        both = jnp.where(jnp.broadcast_to(left_half, one.shape), one, two)
-        return (both * inside).astype(BF16)
+        inside = (column >= 0) & (column < cols)
+        keep_one = jnp.where(left_half & inside, 1.0, 0.0).astype(BF16)
+        keep_two = jnp.where(left_half, 0.0, jnp.where(inside, 1.0, 0.0)).astype(BF16)
+        return one * keep_one + two * keep_two
 
     width = 2 * length
     lanes2 = lax.broadcasted_iota(I32, (1, 2 * width), 1)
@@ -315,8 +327,9 @@
             part = part - jnp.sum(part, axis=0, keepdims=True) * base
             for c in range(2):
                 top = part[:, c * width:(c + 1) * width]
-                low = pltpu.roll(top, length, 1).astype(BF16) * turn_sign
-                stacked.append(jnp.concatenate([top.astype(BF16), low], axis=0))
+                top = top.astype(BF16)
+                low = pltpu.roll(top, length, 1) * turn_sign
+                stacked.append(jnp.concatenate([top, low], axis=0))
         found = []
         for start, size in split(many, 2):
             both = jnp.concatenate(stacked[start:start + size], axis=1)
@@ -353,9 +366,19 @@
             windows.append(anchors_s[c] + shifts_s[1, c, p])
         far[i] = paired(*windows)
 
-    tiles = width // SMAX
-    row_in = lax.broadcasted_iota(I32, (SMAX, width), 0).astype(F32) * 0.5
-    row_in = row_in - (tiles // 2 + 1) * (SMAX // 2)
+    kept, nyquist = rows.shape[0], length // 2
+    tiles = nyquist // SMAX
+    row_in = lax.broadcasted_iota(I32, (SMAX, width), 0)
+    lane_in = lax.broadcasted_iota(I32, (SMAX, width), 1)
+    top = row_in == 0
+    real_weight, imag_weight = jnp.where(top, 0.5, 1.0), jnp.where(top, 0.0, 1.0)
+    edge_weight, flip = jnp.where(top, 1.0, 2.0), jnp.where(lax.rem(row_in, 2) == 0, 1.0, -1.0)
+    corner = jnp.where(top & (lax.rem(lane_in, length) == nyquist), 1.0, 0.0)
+    quarter = lax.rem(lane_in, 4)
+    corner_wave = jnp.where(quarter == 1, -1.0, jnp.where(quarter == 3, 1.0, 0.0))
+
+    def tile(value, t):
+        return value[t * SMAX:(t + 1) * SMAX]
 
     def far_spectra(low, high, stage):
         for i in range(low, high):
@@ -372,32 +395,52 @@
             for c in range(chips):
                 value = far_spec[i * chips + c]
                 crossed.append(spec[day * chips + c] * jnp.concatenate([value, value], axis=1))
-        stacked = []
+        reals, imags = [], []
         for start, size in split(many, 1):
             along = jnp.concatenate(crossed[start:start + size], axis=0)
-            along = jnp.dot(along, back[...], preferred_element_type=F32).astype(BF16)
+            along = jnp.dot(along, back[...], preferred_element_type=F32)
             for w in range(size):
-                part = along[w * length:(w + 1) * length]
-                stacked.append(jnp.concatenate([part[:, :width], part[:, width:]], axis=0))
-        surfaces = []
+                part = along[w * kept:(w + 1) * kept]
+                reals.append(part[:, :width])
+                imags.append(part[:, width:])
+        turned = []
         for start, size in split(many, 1):
-            both = jnp.concatenate(stacked[start:start + size], axis=1)
-            both = jnp.dot(final[...], both, preferred_element_type=F32)
-            surfaces += [both[:, k * width:(k + 1) * width] for k in range(size)]
+            both = []
+            for w in range(start, start + size):
+                last = crossed[w][nyquist:, :width].astype(F32)[:SMAX] * corner
+                last = jnp.sum(last, axis=1, keepdims=True) * corner_wave
+                last = last + tile(imags[w], tiles)
+                imags[w] = jnp.concatenate(
+                    [imags[w][:nyquist], last, imags[w][nyquist + SMAX:]], axis=0
+                )
+                both.append(imags[w].astype(BF16))
+            both = jnp.dot(
+                final[...], jnp.concatenate(both, axis=1), preferred_element_type=F32
+            )
+            turned += [both[:, k * width:(k + 1) * width] for k in range(size)]
         for b in range(high - low):
             for c in range(chips):
                 w = b * chips + c
-                value = surfaces[w]
-                run, ramp = None, None
-                for t in (*range(tiles // 2 - 1, -1, -1), *range(tiles - 1, tiles // 2 - 1, -1)):
-                    energy = value[t * SMAX:(t + 1) * SMAX]
-                    energy = energy * energy
-                    run = energy if run is None else run + energy
-                    ramp = run if ramp is None else ramp + run
+                real, imag, turn = reals[w], imags[w], turned[w]
+                energy, tilt, nodes = None, None, None
+                for t in range(1, tiles):
+                    r, i = tile(real, t), tile(imag, t)
+                    square = r * r + i * i
+                    energy = square if energy is None else energy + square
+                    nodes = r if nodes is None else nodes + r
+                for t in range(tiles + 1):
+                    cross = tile(real, t) * tile(turn, t)
+                    tilt = cross if tilt is None else tilt + cross
+                r, i = tile(real, 0), tile(imag, 0)
+                energy = energy + r * r * real_weight + i * i * imag_weight
+                nodes = 2.0 * nodes + r * edge_weight
+                r, i = tile(real, tiles), tile(imag, tiles)
+                energy = energy + (r * r + i * i) * 0.25
+                nodes = jnp.sum((nodes + r) * flip, axis=0, keepdims=True)
                 at = (c, pl.ds(low + b, 1))
-                sums[at] = jnp.sum(run, axis=0, keepdims=True)
-                weighted = ramp * (SMAX // 2) + run * row_in
-                moments[at] = jnp.sum(weighted, axis=0, keepdims=True)
+                sums[at] = jnp.sum(energy, axis=0, keepdims=True) * (2.0 * width)
+                tilt = jnp.sum(tilt, axis=0, keepdims=True)
+                moments[at] = tilt - nodes * nodes * (0.5 * length)
 
     middle = dates // 2
     if fast:
@@ -435,8 +478,8 @@
                     move.start(("core", 6, link, "rest", k))
 
         early = pairs - 2 * cap
+        hand_on(*range(move.inner))
         far_spectra(0, early, 1)
-        hand_on(*range(move.inner))
         far_centres(0, early)
         move.got(("core", 6))
         move.z_got(6)
@@ -477,6 +520,8 @@
     for x in range(2):
         for c in range(chips):
             offsets_out[x, c:c + 1] = jnp.sum(found[x * chips + c] * pick, axis=0, keepdims=True)
+    if fast:
+        move.left()
     total = partial[...]
     for j, copy in enumerate(copies):
         copy.wait_recv()
@@ -486,8 +531,6 @@
             k = x * chips + c
             value = jnp.sum(inverse[k] * total[k:k + 1], axis=1)[None]
             series_out[x, c:c + 1] = value
-    if fast:
-        move.left()
     for copy in copies:
         copy.wait_send()
 
@@ -550,8 +593,8 @@
             pltpu.VMEM((pairs, length + 2 * SMAX, cols), F32),
             pltpu.VMEM((pairs, length, cols), BF16),
             pltpu.VMEM((dates, length, cols), BF16),
-            pltpu.VMEM((dates * chips, length, 2 * width), BF16),
-            pltpu.VMEM((pairs * chips, length, width), BF16),
+            pltpu.VMEM((dates * chips, tables[1].shape[0], 2 * width), BF16),
+            pltpu.VMEM((pairs * chips, tables[1].shape[0], width), BF16),
             pltpu.VMEM((chips, pairs, width), F32),
             pltpu.VMEM((chips, pairs, width), F32),
             pltpu.VMEM((pairs, pairs), F32),

time: 24 us -> 23 us (0.958)
  Pallas kernels: 22.5 us -> 21.6 us
    pallas_call x1, Pallas kernels: 21.9 us -> 21 us  [body(): pl.pallas_call(functools.partial(pairs_kernel, n, strips, cap), name='pai...]
where the time goes in v3:
time: 23 us; the launch traced here: 22.9 us
  Pallas kernels  21.6 us (94%)
  between operations  1.29 us (6%)
    pallas_call x1, Pallas kernels, body(): pl.pallas_call(functools.partial(pairs_kernel, n, strips, cap), name='pai...  21 us
    pallas_call x1, Pallas kernels, body(): pl.pallas_call(emit_kernel, name='emit', out_shape=(jax.ShapeDtypeStruct(...  0.6 us

profile of v3, /device:TPU:0, one launch (start us, length us, event | category | flops | bytes accessed | tf_op | source)
XLA Modules:
  0.0 22.9 jit_solution(3022365675403213642)
XLA Ops:
  1.3 21.0 %pairs.1 = (f32[2,2,32]{2,1,0:T(2,128)S(1)}, f32[2,2,16]{2,1,0:T(2,128)S(1)}) custom-call(s32[1,32]{1,0:T(1,128)} %bitcast.10, s32[1,32]{1,0:T(1,128)} %bitcast.11, s32[1,32]{1,0:T(1,128)} %bitcast.12, s32[1]{0:T(128)S(6)} %copy.14.count_h, s32[2,2,32]{2,1,0:T(2,128)} %bitcast.9, s32[2]{0:T(128)} %anchors_h.1, bf16[16,8,8,128]{3,2,1,0:T(8,128)(2,1)} %bitcast.7, ...), custom_call_target="tpu_custom_call" | custom-call | tf_op jit(solution)/shard_map/pairs/pallas_call | solution.py:563
  22.3 0.6 %emit.1 = (f32[2,2,32]{2,1,0:T(2,128)}, f32[2,2,16]{2,1,0:T(2,128)}) custom-call(f32[2,2,32]{2,1,0:T(2,128)S(1)} %get-tuple-element.6.offsets, f32[2,2,16]{2,1,0:T(2,128)S(1)} %get-tuple-element.7.series), custom_call_target="tpu_custom_call" | custom-call | tf_op jit(solution)/shard_map/emit/pallas_call | solution.py:612

commit v4 on v3

--- a/solution.py
+++ b/solution.py
@@ -192,7 +192,7 @@
     first_v, block_v, second_v, shifts_v, inverse, forward, rows, back, final,
     grid, late, partial, held_sums,
     local, send, recv,
-    wide, far, near, spec, far_spec, sums, moments, picked, spread_v, columns_v, perm_v,
+    wide, spec, far_spec, sums, moments, picked, spread_v, columns_v, perm_v,
 ):
     groups, dates, _, cols = grid.shape[1:]
     length = SMAX * (groups - 2)
@@ -316,11 +316,14 @@
         step = max(1, many // SPLIT) * size
         return [(at, step) for at in range(0, many * size, step)]
 
-    def spectra(ref, at, many):
-        windows = ref[pl.ds(at, many)].reshape(many * length, cols)
+    def spectra(windows):
+        many = len(windows)
         sections = []
         for start, size in split(many, length):
-            found = jnp.dot(windows[start:start + size], forward[...], preferred_element_type=F32)
+            some = windows[start // length:(start + size) // length]
+            found = jnp.dot(
+                jnp.concatenate(some, axis=0), forward[...], preferred_element_type=F32
+            )
             sections += [found[k:k + length] for k in range(0, size, length)]
         stacked = []
         for part in sections:
@@ -338,10 +341,11 @@
         return found
 
     def near_part(low, high):
+        windows = []
         for d in range(low, high):
             value = grid[own, pl.ds(1, groups - 2), d].astype(F32).reshape(length, cols)
-            near[d] = paired(value, anchors_s[0], value, anchors_s[1])
-        found = spectra(near, low, high - low)
+            windows.append(paired(value, anchors_s[0], value, anchors_s[1]))
+        found = spectra(windows)
         for w in range((high - low) * chips):
             both = jnp.concatenate([found[w], pltpu.roll(found[w], length, 1)], axis=1)
             spec[low * chips + w] = both.astype(BF16)
@@ -351,10 +355,11 @@
         block, day = block_s[0, p], second_s[0, p]
         if fast:
             distance = jnp.bitwise_xor(block, me)
-            value = grid[jnp.where(distance < 6, distance, 0), :, day].astype(F32)
+            value = grid[jnp.where(distance < 6, distance, 0), :, day]
             if stage > 1:
-                other = late[jnp.where(distance == 7, 1, 0), :, day].astype(F32)
+                other = late[jnp.where(distance == 7, 1, 0), :, day]
                 value = jnp.where(distance < 6, value, other)
+            value = value.astype(F32)
         else:
             value = grid[block, :, day].astype(F32)
         wide[i, pl.ds(0, SMAX)] = jnp.where(has_up, value[0], 0.0)
@@ -364,7 +369,7 @@
         for c in range(2):
             windows.append(wide[i, pl.ds(SMAX + shifts_s[0, c, p], length)])
             windows.append(anchors_s[c] + shifts_s[1, c, p])
-        far[i] = paired(*windows)
+        return paired(*windows)
 
     kept, nyquist = rows.shape[0], length // 2
     tiles = nyquist // SMAX
@@ -381,9 +386,7 @@
         return value[t * SMAX:(t + 1) * SMAX]
 
     def far_spectra(low, high, stage):
-        for i in range(low, high):
-            far_cut(i, stage)
-        found = spectra(far, low, high - low)
+        found = spectra([far_cut(i, stage) for i in range(low, high)])
         for w, value in enumerate(found):
             far_spec[low * chips + w] = value.astype(BF16)
 
@@ -591,8 +594,6 @@
             pltpu.SemaphoreType.DMA((kinds,)),
             pltpu.SemaphoreType.DMA((kinds,)),
             pltpu.VMEM((pairs, length + 2 * SMAX, cols), F32),
-            pltpu.VMEM((pairs, length, cols), BF16),
-            pltpu.VMEM((dates, length, cols), BF16),
             pltpu.VMEM((dates * chips, tables[1].shape[0], 2 * width), BF16),
             pltpu.VMEM((pairs * chips, tables[1].shape[0], width), BF16),
             pltpu.VMEM((chips, pairs, width), F32),

time: 23 us -> 22.9 us (level)
  no operation moved by 1% of the time
where the time goes in v4:
time: 22.9 us; the launch traced here: 22.8 us
  Pallas kernels  21.5 us (94%)
  between operations  1.29 us (6%)
    pallas_call x1, Pallas kernels, body(): pl.pallas_call(functools.partial(pairs_kernel, n, strips, cap), name='pai...  20.9 us
    pallas_call x1, Pallas kernels, body(): pl.pallas_call(emit_kernel, name='emit', out_shape=(jax.ShapeDtypeStruct(...  0.6 us

profile of v4, /device:TPU:0, one launch (start us, length us, event | category | flops | bytes accessed | tf_op | source)
XLA Modules:
  0.0 22.8 jit_solution(211256948091664372)
XLA Ops:
  1.3 20.9 %pairs.1 = (f32[2,2,32]{2,1,0:T(2,128)S(1)}, f32[2,2,16]{2,1,0:T(2,128)S(1)}) custom-call(s32[1,32]{1,0:T(1,128)} %bitcast.10, s32[1,32]{1,0:T(1,128)} %bitcast.11, s32[1,32]{1,0:T(1,128)} %bitcast.12, s32[1]{0:T(128)S(6)} %copy.14.count_h, s32[2,2,32]{2,1,0:T(2,128)} %bitcast.9, s32[2]{0:T(128)} %anchors_h.1, bf16[16,8,8,128]{3,2,1,0:T(8,128)(2,1)} %bitcast.7, ...), custom_call_target="tpu_custom_call" | custom-call | tf_op jit(solution)/shard_map/pairs/pallas_call | solution.py:566
  22.2 0.6 %emit.1 = (f32[2,2,32]{2,1,0:T(2,128)}, f32[2,2,16]{2,1,0:T(2,128)}) custom-call(f32[2,2,32]{2,1,0:T(2,128)S(1)} %get-tuple-element.6.offsets, f32[2,2,16]{2,1,0:T(2,128)S(1)} %get-tuple-element.7.series), custom_call_target="tpu_custom_call" | custom-call | tf_op jit(solution)/shard_map/emit/pallas_call | solution.py:613

commit v5 on v4

--- a/solution.py
+++ b/solution.py
@@ -445,6 +445,27 @@
                 tilt = jnp.sum(tilt, axis=0, keepdims=True)
                 moments[at] = tilt - nodes * nodes * (0.5 * length)
 
+    def settle(low, high):
+        many, cells = high - low, 1.0 / (width * width)
+        across = lax.broadcasted_iota(I32, (many, width), 1)
+        across = jnp.where(across < length, across, across - width).astype(F32) * 0.5
+        some = pl.ds(low, many)
+        held_columns, spread, pick = columns_v[some], spread_v[some], picked[some]
+        lives = held_columns[:, 2 * chips:2 * chips + 1] > 0.5
+        sides, places = [None] * (2 * chips), [None] * (2 * chips)
+        for c in range(chips):
+            held = sums[c, some]
+            scale = jnp.sum(held, axis=1, keepdims=True) * cells + 1e-6
+            down_sum = jnp.sum(moments[c, some], axis=1, keepdims=True) * cells
+            side_sum = jnp.sum(held * across, axis=1, keepdims=True) * cells
+            for x, value in enumerate((down_sum, side_sum)):
+                k = x * chips + c
+                found = jnp.where(lives, held_columns[:, k:k + 1] + value / scale, 0.0)
+                sides[k] = jnp.sum(found * spread, axis=0, keepdims=True)
+                places[k] = jnp.sum(found * pick, axis=0, keepdims=True)
+        return sides + places
+
+    settled, settled_to = [], 0
     middle = dates // 2
     if fast:
         near_part(0, middle)
@@ -486,6 +507,7 @@
         far_centres(0, early)
         move.got(("core", 6))
         move.z_got(6)
+        settled, settled_to = [settle(0, early)], early
         far_spectra(early, pairs, 2)
         far_centres(early, pairs)
         sent = move.kinds
@@ -497,32 +519,19 @@
         far_centres(0, pairs)
         sent = 2 + 3 * (n - 1)
 
-    across = lax.broadcasted_iota(I32, (pairs, width), 1)
-    across = jnp.where(across < length, across, across - width).astype(F32) * 0.5
-    cells = 1.0 / (width * width)
-    held_columns = columns_v[...]
-    lives = held_columns[:, 2 * chips:2 * chips + 1] > 0.5
-    spread = spread_v[...]
-    found = [None] * (2 * chips)
-    for c in range(chips):
-        held = sums[c]
-        scale = jnp.sum(held, axis=1, keepdims=True) * cells + 1e-6
-        low = jnp.sum(moments[c], axis=1, keepdims=True) * cells
-        side = jnp.sum(held * across, axis=1, keepdims=True) * cells
-        for x, value in enumerate((low, side)):
-            k = x * chips + c
-            found[k] = jnp.where(lives, held_columns[:, k:k + 1] + value / scale, 0.0)
-            partial[k:k + 1] = jnp.sum(found[k] * spread, axis=0, keepdims=True)
+    settled = settled + [settle(settled_to, pairs)]
+    joined = [sum(row[1:], row[0]) for row in zip(*settled)]
+    for k in range(2 * chips):
+        partial[k:k + 1] = joined[k]
 
     copies = []
     for j in range(1, n):
         where = {"date": lax.rem(me + j, n)}
         copies.append(remote(sent + j - 1, partial, held_sums.at[j - 1], where, send, recv))
         copies[-1].start()
-    pick = picked[...]
     for x in range(2):
         for c in range(chips):
-            offsets_out[x, c:c + 1] = jnp.sum(found[x * chips + c] * pick, axis=0, keepdims=True)
+            offsets_out[x, c:c + 1] = joined[(2 + x) * chips + c]
     if fast:
         move.left()
     total = partial[...]

time: 22.9 us -> 22.9 us (level)
  no operation moved by 1% of the time
where the time goes in v5:
time: 22.9 us; the launch traced here: 22.8 us
  Pallas kernels  21.5 us (94%)
  between operations  1.29 us (6%)
    pallas_call x1, Pallas kernels, body(): pl.pallas_call(functools.partial(pairs_kernel, n, strips, cap), name='pai...  20.9 us
    pallas_call x1, Pallas kernels, body(): pl.pallas_call(emit_kernel, name='emit', out_shape=(jax.ShapeDtypeStruct(...  0.6 us

profile of v5, /device:TPU:0, one launch (start us, length us, event | category | flops | bytes accessed | tf_op | source)
XLA Modules:
  0.0 22.8 jit_solution(2849367660308133535)
XLA Ops:
  1.3 20.9 %pairs.1 = (f32[2,2,32]{2,1,0:T(2,128)S(1)}, f32[2,2,16]{2,1,0:T(2,128)S(1)}) custom-call(s32[1,32]{1,0:T(1,128)} %bitcast.10, s32[1,32]{1,0:T(1,128)} %bitcast.11, s32[1,32]{1,0:T(1,128)} %bitcast.12, s32[1]{0:T(128)S(6)} %copy.14.count_h, s32[2,2,32]{2,1,0:T(2,128)} %bitcast.9, s32[2]{0:T(128)} %anchors_h.1, bf16[16,8,8,128]{3,2,1,0:T(8,128)(2,1)} %bitcast.7, ...), custom_call_target="tpu_custom_call" | custom-call | tf_op jit(solution)/shard_map/pairs/pallas_call | solution.py:575
  22.2 0.6 %emit.1 = (f32[2,2,32]{2,1,0:T(2,128)}, f32[2,2,16]{2,1,0:T(2,128)}) custom-call(f32[2,2,32]{2,1,0:T(2,128)S(1)} %get-tuple-element.6.offsets, f32[2,2,16]{2,1,0:T(2,128)S(1)} %get-tuple-element.7.series), custom_call_target="tpu_custom_call" | custom-call | tf_op jit(solution)/shard_map/emit/pallas_call | solution.py:622

commit v6 on v5

--- a/solution.py
+++ b/solution.py
@@ -229,6 +229,17 @@
     own = 0 if fast else me
     spots = [0, groups - 3, *range(1, groups - 3)]
     mine = [load(img.at[:, g], grid.at[own, 1 + g]) for g in spots]
+    sides = len(side_spots) * (has_up.astype(I32) + has_down.astype(I32))
+    pl.semaphore_wait(barrier, len(greeted) + sides)
+    for copy in mine[:2]:
+        copy.wait()
+    if fast:
+        blocks = [grid.at[d] for d in range(6)] + [late.at[d] for d in range(2)]
+        move = Gather(me, strip, strips, blocks, send, recv)
+        move.start((4, "now_edge"), (2, "now_edge"))
+        move.start((4, "later_edge"), (2, "later_edge"))
+        move.z_start("up", 0)
+        move.z_start("down", 0)
     small = [
         load(a, b)
         for a, b in (
@@ -244,17 +255,6 @@
             (inverse_h, inverse),
         )
     ]
-    sides = len(side_spots) * (has_up.astype(I32) + has_down.astype(I32))
-    pl.semaphore_wait(barrier, len(greeted) + sides)
-    for copy in mine[:2]:
-        copy.wait()
-    if fast:
-        blocks = [grid.at[d] for d in range(6)] + [late.at[d] for d in range(2)]
-        move = Gather(me, strip, strips, blocks, send, recv)
-        move.start((4, "now_edge"), (2, "now_edge"))
-        move.start((4, "later_edge"), (2, "later_edge"))
-        move.z_start("up", 0)
-        move.z_start("down", 0)
     for copy in mine[2:]:
         copy.wait()
     if fast:

time: 22.9 us -> 23 us (level)
  no operation moved by 1% of the time
where the time goes in v6:
time: 23 us; the launch traced here: 22.8 us
  Pallas kernels  21.5 us (93%)
  between operations  1.29 us (6%)
    pallas_call x1, Pallas kernels, body(): pl.pallas_call(functools.partial(pairs_kernel, n, strips, cap), name='pai...  20.9 us
    pallas_call x1, Pallas kernels, body(): pl.pallas_call(emit_kernel, name='emit', out_shape=(jax.ShapeDtypeStruct(...  0.6 us

profile of v6, /device:TPU:0, one launch (start us, length us, event | category | flops | bytes accessed | tf_op | source)
XLA Modules:
  0.0 22.8 jit_solution(16504598940144654566)
XLA Ops:
  1.3 20.9 %pairs.1 = (f32[2,2,32]{2,1,0:T(2,128)S(1)}, f32[2,2,16]{2,1,0:T(2,128)S(1)}) custom-call(s32[1,32]{1,0:T(1,128)} %bitcast.10, s32[1,32]{1,0:T(1,128)} %bitcast.11, s32[1,32]{1,0:T(1,128)} %bitcast.12, s32[1]{0:T(128)S(6)} %copy.14.count_h, s32[2,2,32]{2,1,0:T(2,128)} %bitcast.9, s32[2]{0:T(128)} %anchors_h.1, bf16[16,8,8,128]{3,2,1,0:T(8,128)(2,1)} %bitcast.7, ...), custom_call_target="tpu_custom_call" | custom-call | tf_op jit(solution)/shard_map/pairs/pallas_call | solution.py:575
  22.2 0.6 %emit.1 = (f32[2,2,32]{2,1,0:T(2,128)}, f32[2,2,16]{2,1,0:T(2,128)}) custom-call(f32[2,2,32]{2,1,0:T(2,128)S(1)} %get-tuple-element.6.offsets, f32[2,2,16]{2,1,0:T(2,128)S(1)} %get-tuple-element.7.series), custom_call_target="tpu_custom_call" | custom-call | tf_op jit(solution)/shard_map/emit/pallas_call | solution.py:622
